TPU v7x, 512 devices: a whole 4x4x16 slice. The times are simulated.
512 devices in a mesh: row: 32 (over x, y, core), col: 16 (over z).
Axes of the slice: x: 4, y: 4, z: 16, core: 2. Of those that a mesh axis runs over, the one named last changes fastest.
Arguments:
- similarity: float32 [8192, 8192], P('row', 'col'), may hold values from 0.1 to 500
- pattern: int32 [32, 32], P('row', 'col'), may hold values from 0 to 1, as said below
Outputs:
- clustered: float32 [8192, 8192], P('row', 'col')
Inputs may be any that keep to these rules, and one draw needn't show every extreme that they name: `pattern`: every diagonal tile (g, g) is stored.
All inputs are finite; a program needn't handle non-finite values.
Results may differ from a plain program's by a relative error of at most 0.0003.
Values may be sent and summed in bfloat16 or wider, within the bound.
A program may use at most 64 MiB of HBM per device.

v0:
```python
import jax
import jax.numpy as jnp
from jax import lax
from jax.sharding import PartitionSpec as P

TILE = 256


def spread(pattern):
    rows, cols = pattern.shape
    values = pattern.astype(jnp.float32)
    return jnp.broadcast_to(values[:, None, :, None], (rows, TILE, cols, TILE)).reshape(
        rows * TILE, cols * TILE
    )


def tile_sum(left_part, right_part):
    return jnp.dot(left_part, right_part, preferred_element_type=jnp.float32)


def product(operand):
    left = lax.all_gather(operand, "col", axis=1, tiled=True)
    return tile_sum(left, lax.all_gather(operand, "row", axis=0, tiled=True))


def shards(similarity, pattern):
    cells = spread(pattern)
    total_rows = similarity.shape[0] * lax.axis_size("row")
    held = similarity * cells
    start_total = lax.psum(jnp.sum(held, axis=0), "row")
    matrix = held * (total_rows / start_total)[None, :]
    operand = matrix.astype(jnp.bfloat16)
    expanded = product(operand) * cells
    inflated = expanded * expanded
    sums = lax.psum(jnp.sum(inflated, axis=0), "row")
    matrix = inflated * (total_rows / sums)[None, :]
    return matrix


def solution(mesh):
    placed = (P("row", "col"), P("row", "col"))
    return jax.shard_map(
        shards, mesh=mesh, in_specs=placed, out_specs=P("row", "col"), check_vma=False
    )
```

profile of v0, /device:TPU:32, one launch (start us, length us, event | category | flops | bytes accessed | tf_op | source)
XLA Modules:
  0.0 303.6 jit_solution(1512720498870579981)
XLA Ops:
  6.5 0.0 all-gather.3.cloned.1.call-start
  6.5 0.7 convert_bitcast_fusion
  7.2 0.1 broadcast_bitcast_fusion
  7.3 1.1 multiply_reduce_fusion
  8.4 67.3 %psum.14 = f32[512]{0:T(512)S(1)} all-reduce(f32[512]{0:T(512)S(1)} %multiply_reduce_fusion), channel_id=1, replica_groups=mesh['row'=32,'col'=16] {'row'}, use_global_device_ids=true, to_apply=%region_1.0 | all-reduce | flops 512 | bytes 4096 | tf_op jit(solution)/shard_map/psum | solution.py:30
  75.7 1.8 multiply_convert_fusion
  77.5 0.0 all-gather.3.cloned.1.call-update
  77.5 0.0 all-gather.5.cloned.1.call-start
  77.6 0.7 all-gather.5.cloned.1.call-update
  78.3 77.1 %all-gather.3.cloned.1.call-done = bf16[256,8192]{1,0:T(8,128)(2,1)} async-done(((bf16[256,512]{1,0:T(8,128)(2,1)}), bf16[256,8192]{1,0:T(8,128)(2,1)}) %all-gather.3.cloned.1.call-update) | async-done | bytes 4194320 | tf_op jit(solution)/shard_map/all_gather | solution.py:22
  155.3 68.1 %all-gather.5.cloned.1.call-done = bf16[8192,512]{1,0:T(8,128)(2,1)} async-done(((bf16[256,512]{1,0:T(8,128)(2,1)}), bf16[8192,512]{1,0:T(8,128)(2,1)}) %all-gather.5.cloned.1.call-update) | async-done | bytes 8388624 | tf_op jit(solution)/shard_map/all_gather | solution.py:23
  223.4 7.0 %fusion.1 = (f32[512]{0:T(512)S(1)}, f32[256,512]{1,0:T(8,128)S(1)}) fusion(f32[512]{0:T(512)S(1)} %bitcast.9, bf16[256,8192]{1,0:T(8,128)(2,1)} %all-gather.3.cloned.1.call-done, bf16[8192,512]{1,0:T(8,128)(2,1)} %all-gather.5.cloned.1.call-done), kind=kOutput, calls=%fused_computation.9 | convolution fusion | flops 2147876352 | bytes 13111296 | tf_op jit(solution)/shard_map/dot_general | solution.py:18
  230.4 65.5 %psum.15 = f32[512]{0:T(512)S(1)} all-reduce(f32[512]{0:T(512)S(1)} %get-tuple-element.5), channel_id=1, replica_groups=mesh['row'=32,'col'=16] {'row'}, use_global_device_ids=true, to_apply=%region_3.0 | all-reduce | flops 512 | bytes 4096 | tf_op jit(solution)/shard_map/psum | solution.py:35
  295.9 0.9 broadcast_multiply_fusion
  (3 shorter events, 0.0 us)
Async XLA Ops:
  6.5 148.8 %all-gather.3.cloned.1.call-start = ((), (), s32[]{:S(2)}) async-start(), calls=%async_computation | async-start | bytes 4456448 | tf_op jit(solution)/shard_map/all_gather | solution.py:22
  77.5 145.9 %all-gather.5.cloned.1.call-start = ((), (), s32[]{:S(2)}) async-start(), calls=%async_computation.1 | async-start | bytes 8650752 | tf_op jit(solution)/shard_map/all_gather | solution.py:23
Sparse Core Ops, SparseCore 0:
  77.6 77.6 all-gather.2
  158.5 64.8 all-gather.4
where the time goes:
time: 304 us
  waiting for transfers between devices  146 us (48%)
  blocking collectives  133 us (44%)
  between operations  13.4 us (4%)
  matrix products  6.99 us (2%)
  other arithmetic  4.45 us (1%)
    all_gather x1, waiting for transfers between devices, product(): left = lax.all_gather(operand, 'col', axis=1, tiled=True)  77.1 us
    all_gather x1, waiting for transfers between devices, product(): return tile_sum(left, lax.all_gather(operand, 'row', axis=0, tiled=True))  68.1 us
    psum x1, blocking collectives, shards(): start_total = lax.psum(jnp.sum(held, axis=0), 'row')  67.3 us
    psum x1, blocking collectives, shards(): sums = lax.psum(jnp.sum(inflated, axis=0), 'row')  65.5 us
    dot_general x1, matrix products, tile_sum(): return jnp.dot(left_part, right_part, preferred_element_type=jnp.float32)  6.99 us
  transfers between devices with their start and end apart: 2, of which 2 were waited for; matrix products, arithmetic and copies ran while one was open for 0% of the time, Pallas kernels for 0%

commit v1 on v0

--- a/solution.py
+++ b/solution.py
@@ -19,7 +19,13 @@
 
 
 def product(operand):
-    left = lax.all_gather(operand, "col", axis=1, tiled=True)
+    count = lax.axis_size("col")
+    moving, blocks = (operand, [operand])
+    for _ in range(count - 1):
+        moving = lax.ppermute(moving, "col", [(i, (i + 1) % count) for i in range(count)])
+        blocks.insert(0, moving)
+    flat = jnp.concatenate(blocks, axis=1)
+    left = jnp.roll(flat, (lax.axis_index("col") + 1) * operand.shape[1], axis=1)
     return tile_sum(left, lax.all_gather(operand, "row", axis=0, tiled=True))
 
 

time: 304 us -> 351 us (1.15)
  the two profiles are of different devices: /device:TPU:32 before, /device:TPU:1 now
where the time goes in v1:
time: 351 us; the launch traced here: 350 us
  blocking collectives  152 us (43%)
  waiting for transfers between devices  113 us (32%)
  local copies, waits for them, and re-layouts  29.6 us (8%)
  starting transfers between devices  28.6 us (8%)
  between operations  13.6 us (4%)
  matrix products  7 us (2%)
  other arithmetic  6.07 us (2%)
    ppermute x15, waiting for transfers between devices, product(): lax.ppermute(moving, 'col', [(i, (i + 1) % count) for i in range(count)])  113 us
    psum x1, blocking collectives, shards(): sums = lax.psum(jnp.sum(inflated, axis=0), 'row')  82.9 us
    psum x1, blocking collectives, shards(): start_total = lax.psum(jnp.sum(held, axis=0), 'row')  68.9 us
    unnamed x42, local copies, waits for them, and re-layouts  29.6 us
    ppermute x15, starting transfers between devices, product(): lax.ppermute(moving, 'col', [(i, (i + 1) % count) for i in range(count)])  28.6 us
  transfers between devices with their start and end apart: 16, of which 15 were waited for; matrix products, arithmetic and copies ran while one was open for 8% of the time, Pallas kernels for 0%

profile of v1, /device:TPU:1, one launch (start us, length us, event | category | flops | bytes accessed | tf_op | source)
XLA Modules:
  0.0 349.8 jit_solution(1014179625667337575)
XLA Ops:
  8.4 68.9 %psum.14 = f32[512]{0:T(512)S(1)} all-reduce(f32[512]{0:T(512)S(1)} %multiply_reduce_fusion), channel_id=1, replica_groups=mesh['row'=32,'col'=16] {'row'}, use_global_device_ids=true, to_apply=%region_1.0 | all-reduce | flops 512 | bytes 4096 | tf_op jit(solution)/shard_map/psum | solution.py:36
  79.2 1.9 collective-permute-start
  81.1 8.0 %collective-permute-done = bf16[256,512]{1,0:T(8,128)(2,1)S(1)} collective-permute-done((bf16[256,512]{1,0:T(8,128)(2,1)}, bf16[256,512]{1,0:T(8,128)(2,1)S(1)}, u32[]{:S(2)}, u32[]{:S(2)}) %collective-permute-start) | collective-permute-done | bytes 262176 | tf_op jit(solution)/shard_map/ppermute | solution.py:25
  89.2 1.9 collective-permute-start.1
  91.1 6.4 %collective-permute-done.1 = bf16[256,512]{1,0:T(8,128)(2,1)S(1)} collective-permute-done((bf16[256,512]{1,0:T(8,128)(2,1)S(1)}, bf16[256,512]{1,0:T(8,128)(2,1)S(1)}, u32[]{:S(2)}, u32[]{:S(2)}) %collective-permute-start.1) | collective-permute-done | bytes 262176 | tf_op jit(solution)/shard_map/ppermute | solution.py:25
  97.5 1.9 collective-permute-start.2
  99.4 7.2 %collective-permute-done.2 = bf16[256,512]{1,0:T(8,128)(2,1)S(1)} collective-permute-done((bf16[256,512]{1,0:T(8,128)(2,1)S(1)}, bf16[256,512]{1,0:T(8,128)(2,1)S(1)}, u32[]{:S(2)}, u32[]{:S(2)}) %collective-permute-start.2) | collective-permute-done | bytes 262176 | tf_op jit(solution)/shard_map/ppermute | solution.py:25
  106.6 1.9 collective-permute-start.3
  108.5 8.6 %collective-permute-done.3 = bf16[256,512]{1,0:T(8,128)(2,1)S(1)} collective-permute-done((bf16[256,512]{1,0:T(8,128)(2,1)S(1)}, bf16[256,512]{1,0:T(8,128)(2,1)S(1)}, u32[]{:S(2)}, u32[]{:S(2)}) %collective-permute-start.3) | collective-permute-done | bytes 262176 | tf_op jit(solution)/shard_map/ppermute | solution.py:25
  117.1 1.9 collective-permute-start.4
  119.0 9.1 %collective-permute-done.4 = bf16[256,512]{1,0:T(8,128)(2,1)S(1)} collective-permute-done((bf16[256,512]{1,0:T(8,128)(2,1)S(1)}, bf16[256,512]{1,0:T(8,128)(2,1)S(1)}, u32[]{:S(2)}, u32[]{:S(2)}) %collective-permute-start.4) | collective-permute-done | bytes 262176 | tf_op jit(solution)/shard_map/ppermute | solution.py:25
  128.1 1.9 collective-permute-start.5
  130.0 8.2 %collective-permute-done.5 = bf16[256,512]{1,0:T(8,128)(2,1)S(1)} collective-permute-done((bf16[256,512]{1,0:T(8,128)(2,1)S(1)}, bf16[256,512]{1,0:T(8,128)(2,1)S(1)}, u32[]{:S(2)}, u32[]{:S(2)}) %collective-permute-start.5) | collective-permute-done | bytes 262176 | tf_op jit(solution)/shard_map/ppermute | solution.py:25
  138.2 1.9 collective-permute-start.6
  140.2 7.3 %collective-permute-done.6 = bf16[256,512]{1,0:T(8,128)(2,1)S(1)} collective-permute-done((bf16[256,512]{1,0:T(8,128)(2,1)S(1)}, bf16[256,512]{1,0:T(8,128)(2,1)S(1)}, u32[]{:S(2)}, u32[]{:S(2)}) %collective-permute-start.6) | collective-permute-done | bytes 262176 | tf_op jit(solution)/shard_map/ppermute | solution.py:25
  147.5 1.9 collective-permute-start.7
  149.4 6.4 %collective-permute-done.7 = bf16[256,512]{1,0:T(8,128)(2,1)S(1)} collective-permute-done((bf16[256,512]{1,0:T(8,128)(2,1)S(1)}, bf16[256,512]{1,0:T(8,128)(2,1)S(1)}, u32[]{:S(2)}, u32[]{:S(2)}) %collective-permute-start.7) | collective-permute-done | bytes 262176 | tf_op jit(solution)/shard_map/ppermute | solution.py:25
  155.8 1.9 collective-permute-start.8
  157.7 6.4 %collective-permute-done.8 = bf16[256,512]{1,0:T(8,128)(2,1)S(1)} collective-permute-done((bf16[256,512]{1,0:T(8,128)(2,1)S(1)}, bf16[256,512]{1,0:T(8,128)(2,1)S(1)}, u32[]{:S(2)}, u32[]{:S(2)}) %collective-permute-start.8) | collective-permute-done | bytes 262176 | tf_op jit(solution)/shard_map/ppermute | solution.py:25
  164.1 1.9 collective-permute-start.9
  166.0 6.4 %collective-permute-done.9 = bf16[256,512]{1,0:T(8,128)(2,1)S(1)} collective-permute-done((bf16[256,512]{1,0:T(8,128)(2,1)S(1)}, bf16[256,512]{1,0:T(8,128)(2,1)S(1)}, u32[]{:S(2)}, u32[]{:S(2)}) %collective-permute-start.9) | collective-permute-done | bytes 262176 | tf_op jit(solution)/shard_map/ppermute | solution.py:25
  172.4 1.9 collective-permute-start.10
  174.3 6.4 %collective-permute-done.10 = bf16[256,512]{1,0:T(8,128)(2,1)S(1)} collective-permute-done((bf16[256,512]{1,0:T(8,128)(2,1)S(1)}, bf16[256,512]{1,0:T(8,128)(2,1)S(1)}, u32[]{:S(2)}, u32[]{:S(2)}) %collective-permute-start.10) | collective-permute-done | bytes 262176 | tf_op jit(solution)/shard_map/ppermute | solution.py:25
  180.7 1.9 collective-permute-start.11
  182.7 7.4 %collective-permute-done.11 = bf16[256,512]{1,0:T(8,128)(2,1)S(1)} collective-permute-done((bf16[256,512]{1,0:T(8,128)(2,1)S(1)}, bf16[256,512]{1,0:T(8,128)(2,1)S(1)}, u32[]{:S(2)}, u32[]{:S(2)}) %collective-permute-start.11) | collective-permute-done | bytes 262176 | tf_op jit(solution)/shard_map/ppermute | solution.py:25
  192.7 7.8 %collective-permute-done.12 = bf16[256,512]{1,0:T(8,128)(2,1)S(1)} collective-permute-done((bf16[256,512]{1,0:T(8,128)(2,1)S(1)}, bf16[256,512]{1,0:T(8,128)(2,1)S(1)}, u32[]{:S(2)}, u32[]{:S(2)}) %collective-permute-start.12) | collective-permute-done | bytes 262176 | tf_op jit(solution)/shard_map/ppermute | solution.py:25
  201.1 1.9 collective-permute-start.13
  203.0 8.2 %collective-permute-done.13 = bf16[256,512]{1,0:T(8,128)(2,1)} collective-permute-done((bf16[256,512]{1,0:T(8,128)(2,1)S(1)}, bf16[256,512]{1,0:T(8,128)(2,1)}, u32[]{:S(2)}, u32[]{:S(2)}) %collective-permute-start.13) | collective-permute-done | bytes 262176 | tf_op jit(solution)/shard_map/ppermute | solution.py:25
  211.3 1.9 collective-permute-start.14
  213.2 9.3 %collective-permute-done.14 = bf16[256,512]{1,0:T(8,128)(2,1)} collective-permute-done((bf16[256,512]{1,0:T(8,128)(2,1)}, bf16[256,512]{1,0:T(8,128)(2,1)}, u32[]{:S(2)}, u32[]{:S(2)}) %collective-permute-start.14) | collective-permute-done | bytes 262176 | tf_op jit(solution)/shard_map/ppermute | solution.py:25
  252.2 7.0 %fusion.9 = (f32[512]{0:T(512)S(1)}, f32[256,512]{1,0:T(8,128)S(1)}) fusion(f32[512]{0:T(512)S(1)} %bitcast.10, bf16[8192,512]{1,0:T(8,128)(2,1)} %all-gather.2.cloned.1.call-done, bf16[256,16384]{1,0:T(8,128)(2,1)} %constant_dynamic-update-slice_fusion, s32[]{:T(128)S(6)} %select_n.14), kind=kOutput, calls=%fused_computation.44 | convolution fusion | flops 2147876352 | bytes 13111300 | tf_op jit(solution)/shard_map/dot_general | solution.py:18
  259.2 82.9 %psum.15 = f32[512]{0:T(512)S(1)} all-reduce(f32[512]{0:T(512)S(1)} %get-tuple-element.5), channel_id=1, replica_groups=mesh['row'=32,'col'=16] {'row'}, use_global_device_ids=true, to_apply=%region_3.4 | all-reduce | flops 512 | bytes 4096 | tf_op jit(solution)/shard_map/psum | solution.py:41
  (54 shorter events, 37.6 us)
Async XLA Ops:
  6.5 231.0 %copy-start = (f32[256,512]{1,0:T(8,128)S(1)}, f32[256,512]{1,0:T(8,128)}, u32[]{:S(2)}) copy-start(f32[256,512]{1,0:T(8,128)} %param.2) | copy-start | bytes 1572868
  6.5 245.7 %all-gather.2.cloned.1.call-start = ((), (), s32[]{:S(2)}) async-start(), calls=%async_computation | async-start | bytes 8650752 | tf_op jit(solution)/shard_map/all_gather | solution.py:29
  79.2 10.0 %collective-permute-start = (bf16[256,512]{1,0:T(8,128)(2,1)}, bf16[256,512]{1,0:T(8,128)(2,1)S(1)}, u32[]{:S(2)}, u32[]{:S(2)}) collective-permute-start(bf16[256,512]{1,0:T(8,128)(2,1)} %multiply_convert_fusion), channel_id=1, source_target_pairs={{0,1},{1,2},{2,3},{3,4},{4,5},{5,6},{6,7},{7,8},{8,9},{9,10},{10,1... | collective-permute-start | bytes 786440 | tf_op jit(solution)/shard_map/ppermute | solution.py:25
  89.2 8.3 %collective-permute-start.1 = (bf16[256,512]{1,0:T(8,128)(2,1)S(1)}, bf16[256,512]{1,0:T(8,128)(2,1)S(1)}, u32[]{:S(2)}, u32[]{:S(2)}) collective-permute-start(bf16[256,512]{1,0:T(8,128)(2,1)S(1)} %collective-permute-done), channel_id=1, source_target_pairs={{0,1},{1,2},{2,3},{3,4},{4,5},{5,6},{6,7},{7,8},{8,9},{9,10},{10,1... | collective-permute-start | bytes 786440 | tf_op jit(solution)/shard_map/ppermute | solution.py:25
  97.5 9.2 %collective-permute-start.2 = (bf16[256,512]{1,0:T(8,128)(2,1)S(1)}, bf16[256,512]{1,0:T(8,128)(2,1)S(1)}, u32[]{:S(2)}, u32[]{:S(2)}) collective-permute-start(bf16[256,512]{1,0:T(8,128)(2,1)S(1)} %collective-permute-done.1), channel_id=1, source_target_pairs={{0,1},{1,2},{2,3},{3,4},{4,5},{5,6},{6,7},{7,8},{8,9},{9,10},{10,1... | collective-permute-start | bytes 786440 | tf_op jit(solution)/shard_map/ppermute | solution.py:25
  106.6 10.5 %collective-permute-start.3 = (bf16[256,512]{1,0:T(8,128)(2,1)S(1)}, bf16[256,512]{1,0:T(8,128)(2,1)S(1)}, u32[]{:S(2)}, u32[]{:S(2)}) collective-permute-start(bf16[256,512]{1,0:T(8,128)(2,1)S(1)} %collective-permute-done.2), channel_id=1, source_target_pairs={{0,1},{1,2},{2,3},{3,4},{4,5},{5,6},{6,7},{7,8},{8,9},{9,10},{10,1... | collective-permute-start | bytes 786440 | tf_op jit(solution)/shard_map/ppermute | solution.py:25
  117.1 11.0 %collective-permute-start.4 = (bf16[256,512]{1,0:T(8,128)(2,1)S(1)}, bf16[256,512]{1,0:T(8,128)(2,1)S(1)}, u32[]{:S(2)}, u32[]{:S(2)}) collective-permute-start(bf16[256,512]{1,0:T(8,128)(2,1)S(1)} %collective-permute-done.3), channel_id=1, source_target_pairs={{0,1},{1,2},{2,3},{3,4},{4,5},{5,6},{6,7},{7,8},{8,9},{9,10},{10,1... | collective-permute-start | bytes 786440 | tf_op jit(solution)/shard_map/ppermute | solution.py:25
  128.1 10.1 %collective-permute-start.5 = (bf16[256,512]{1,0:T(8,128)(2,1)S(1)}, bf16[256,512]{1,0:T(8,128)(2,1)S(1)}, u32[]{:S(2)}, u32[]{:S(2)}) collective-permute-start(bf16[256,512]{1,0:T(8,128)(2,1)S(1)} %collective-permute-done.4), channel_id=1, source_target_pairs={{0,1},{1,2},{2,3},{3,4},{4,5},{5,6},{6,7},{7,8},{8,9},{9,10},{10,1... | collective-permute-start | bytes 786440 | tf_op jit(solution)/shard_map/ppermute | solution.py:25
  138.2 9.2 %collective-permute-start.6 = (bf16[256,512]{1,0:T(8,128)(2,1)S(1)}, bf16[256,512]{1,0:T(8,128)(2,1)S(1)}, u32[]{:S(2)}, u32[]{:S(2)}) collective-permute-start(bf16[256,512]{1,0:T(8,128)(2,1)S(1)} %collective-permute-done.5), channel_id=1, source_target_pairs={{0,1},{1,2},{2,3},{3,4},{4,5},{5,6},{6,7},{7,8},{8,9},{9,10},{10,1... | collective-permute-start | bytes 786440 | tf_op jit(solution)/shard_map/ppermute | solution.py:25
  147.5 8.3 %collective-permute-start.7 = (bf16[256,512]{1,0:T(8,128)(2,1)S(1)}, bf16[256,512]{1,0:T(8,128)(2,1)S(1)}, u32[]{:S(2)}, u32[]{:S(2)}) collective-permute-start(bf16[256,512]{1,0:T(8,128)(2,1)S(1)} %collective-permute-done.6), channel_id=1, source_target_pairs={{0,1},{1,2},{2,3},{3,4},{4,5},{5,6},{6,7},{7,8},{8,9},{9,10},{10,1... | collective-permute-start | bytes 786440 | tf_op jit(solution)/shard_map/ppermute | solution.py:25
  155.8 8.3 %collective-permute-start.8 = (bf16[256,512]{1,0:T(8,128)(2,1)S(1)}, bf16[256,512]{1,0:T(8,128)(2,1)S(1)}, u32[]{:S(2)}, u32[]{:S(2)}) collective-permute-start(bf16[256,512]{1,0:T(8,128)(2,1)S(1)} %collective-permute-done.7), channel_id=1, source_target_pairs={{0,1},{1,2},{2,3},{3,4},{4,5},{5,6},{6,7},{7,8},{8,9},{9,10},{10,1... | collective-permute-start | bytes 786440 | tf_op jit(solution)/shard_map/ppermute | solution.py:25
  164.1 8.3 %collective-permute-start.9 = (bf16[256,512]{1,0:T(8,128)(2,1)S(1)}, bf16[256,512]{1,0:T(8,128)(2,1)S(1)}, u32[]{:S(2)}, u32[]{:S(2)}) collective-permute-start(bf16[256,512]{1,0:T(8,128)(2,1)S(1)} %collective-permute-done.8), channel_id=1, source_target_pairs={{0,1},{1,2},{2,3},{3,4},{4,5},{5,6},{6,7},{7,8},{8,9},{9,10},{10,1... | collective-permute-start | bytes 786440 | tf_op jit(solution)/shard_map/ppermute | solution.py:25
  172.4 8.3 %collective-permute-start.10 = (bf16[256,512]{1,0:T(8,128)(2,1)S(1)}, bf16[256,512]{1,0:T(8,128)(2,1)S(1)}, u32[]{:S(2)}, u32[]{:S(2)}) collective-permute-start(bf16[256,512]{1,0:T(8,128)(2,1)S(1)} %collective-permute-done.9), channel_id=1, source_target_pairs={{0,1},{1,2},{2,3},{3,4},{4,5},{5,6},{6,7},{7,8},{8,9},{9,10},{10,1... | collective-permute-start | bytes 786440 | tf_op jit(solution)/shard_map/ppermute | solution.py:25
  180.7 9.3 %collective-permute-start.11 = (bf16[256,512]{1,0:T(8,128)(2,1)S(1)}, bf16[256,512]{1,0:T(8,128)(2,1)S(1)}, u32[]{:S(2)}, u32[]{:S(2)}) collective-permute-start(bf16[256,512]{1,0:T(8,128)(2,1)S(1)} %collective-permute-done.10), channel_id=1, source_target_pairs={{0,1},{1,2},{2,3},{3,4},{4,5},{5,6},{6,7},{7,8},{8,9},{9,10},{10,1... | collective-permute-start | bytes 786440 | tf_op jit(solution)/shard_map/ppermute | solution.py:25
  190.0 0.7 copy-start.1
  190.8 9.7 %collective-permute-start.12 = (bf16[256,512]{1,0:T(8,128)(2,1)S(1)}, bf16[256,512]{1,0:T(8,128)(2,1)S(1)}, u32[]{:S(2)}, u32[]{:S(2)}) collective-permute-start(bf16[256,512]{1,0:T(8,128)(2,1)S(1)} %collective-permute-done.11), channel_id=1, source_target_pairs={{0,1},{1,2},{2,3},{3,4},{4,5},{5,6},{6,7},{7,8},{8,9},{9,10},{10,1... | collective-permute-start | bytes 786440 | tf_op jit(solution)/shard_map/ppermute | solution.py:25
  200.4 0.7 copy-start.3
  201.1 10.2 %collective-permute-start.13 = (bf16[256,512]{1,0:T(8,128)(2,1)S(1)}, bf16[256,512]{1,0:T(8,128)(2,1)}, u32[]{:S(2)}, u32[]{:S(2)}) collective-permute-start(bf16[256,512]{1,0:T(8,128)(2,1)S(1)} %collective-permute-done.12), channel_id=1, source_target_pairs={{0,1},{1,2},{2,3},{3,4},{4,5},{5,6},{6,7},{7,8},{8,9},{9,10},{10,1... | collective-permute-start | bytes 786440 | tf_op jit(solution)/shard_map/ppermute | solution.py:25
  211.3 11.2 %collective-permute-start.14 = (bf16[256,512]{1,0:T(8,128)(2,1)}, bf16[256,512]{1,0:T(8,128)(2,1)}, u32[]{:S(2)}, u32[]{:S(2)}) collective-permute-start(bf16[256,512]{1,0:T(8,128)(2,1)} %collective-permute-done.13), channel_id=1, source_target_pairs={{0,1},{1,2},{2,3},{3,4},{4,5},{5,6},{6,7},{7,8},{8,9},{9,10},{10,1... | collective-permute-start | bytes 786440 | tf_op jit(solution)/shard_map/ppermute | solution.py:25
  213.2 28.4 %copy-start.4 = (bf16[256,512]{1,0:T(8,128)(2,1)S(1)}, bf16[256,512]{1,0:T(8,128)(2,1)}, u32[]{:S(2)}) copy-start(bf16[256,512]{1,0:T(8,128)(2,1)} %copy-done.3) | copy-start | bytes 786436
  213.2 29.2 %copy-start.2 = (bf16[256,512]{1,0:T(8,128)(2,1)S(1)}, bf16[256,512]{1,0:T(8,128)(2,1)}, u32[]{:S(2)}) copy-start(bf16[256,512]{1,0:T(8,128)(2,1)} %copy-done.1) | copy-start | bytes 786436
Sparse Core Ops, SparseCore 0:
  79.3 67.2 all-gather.1

commit v2 on v0

--- a/solution.py
+++ b/solution.py
@@ -4,6 +4,11 @@
 from jax.sharding import PartitionSpec as P
 
 TILE = 256
+
+
+def summed_here(x, axis):
+    parts = lax.all_gather(x, axis)
+    return jnp.sum(parts, axis=0)
 
 
 def spread(pattern):
@@ -32,7 +37,7 @@
     operand = matrix.astype(jnp.bfloat16)
     expanded = product(operand) * cells
     inflated = expanded * expanded
-    sums = lax.psum(jnp.sum(inflated, axis=0), "row")
+    sums = summed_here(jnp.sum(inflated, axis=0), "row")
     matrix = inflated * (total_rows / sums)[None, :]
     return matrix
 

time: 304 us -> 264 us (0.87)
  the two profiles are of different devices: /device:TPU:32 before, /device:TPU:1 now
where the time goes in v2:
time: 264 us
  waiting for transfers between devices  146 us (55%)
  blocking collectives  92.8 us (35%)
  between operations  13.4 us (5%)
  matrix products  7 us (3%)
  other arithmetic  4.51 us (2%)
    all_gather x1, waiting for transfers between devices, product(): return tile_sum(left, lax.all_gather(operand, 'row', axis=0, tiled=True))  77.2 us
    psum x1, blocking collectives, shards(): start_total = lax.psum(jnp.sum(held, axis=0), 'row')  68.9 us
    all_gather x1, waiting for transfers between devices, product(): left = lax.all_gather(operand, 'col', axis=1, tiled=True)  68 us
    all_gather x1, blocking collectives, summed_here(): parts = lax.all_gather(x, axis)  23.9 us
    dot_general x1, matrix products, tile_sum(): return jnp.dot(left_part, right_part, preferred_element_type=jnp.float32)  7 us
  transfers between devices with their start and end apart: 2, of which 2 were waited for; matrix products, arithmetic and copies ran while one was open for 0% of the time, Pallas kernels for 0%

profile of v2, /device:TPU:1, one launch (start us, length us, event | category | flops | bytes accessed | tf_op | source)
XLA Modules:
  0.0 263.7 jit_solution(3359226580402586293)
XLA Ops:
  6.5 0.0 all-gather.5.cloned.1.call-start
  6.5 0.7 convert_bitcast_fusion
  7.2 0.1 broadcast_bitcast_fusion
  7.3 1.1 multiply_reduce_fusion
  8.4 68.9 %psum.7 = f32[512]{0:T(512)S(1)} all-reduce(f32[512]{0:T(512)S(1)} %multiply_reduce_fusion), channel_id=1, replica_groups=mesh['row'=32,'col'=16] {'row'}, use_global_device_ids=true, to_apply=%region_1.0 | all-reduce | flops 512 | bytes 4096 | tf_op jit(solution)/shard_map/psum | solution.py:35
  77.3 1.8 multiply_convert_fusion
  79.1 0.0 all-gather.5.cloned.1.call-update
  79.1 0.0 all-gather.7.cloned.1.call-start
  79.2 0.7 all-gather.7.cloned.1.call-update
  79.9 68.0 %all-gather.5.cloned.1.call-done = bf16[256,8192]{1,0:T(8,128)(2,1)} async-done(((bf16[256,512]{1,0:T(8,128)(2,1)}), bf16[256,8192]{1,0:T(8,128)(2,1)}) %all-gather.5.cloned.1.call-update) | async-done | bytes 4194320 | tf_op jit(solution)/shard_map/all_gather | solution.py:27
  147.8 77.2 %all-gather.7.cloned.1.call-done = bf16[8192,512]{1,0:T(8,128)(2,1)} async-done(((bf16[256,512]{1,0:T(8,128)(2,1)}), bf16[8192,512]{1,0:T(8,128)(2,1)}) %all-gather.7.cloned.1.call-update) | async-done | bytes 8388624 | tf_op jit(solution)/shard_map/all_gather | solution.py:28
  225.0 7.0 %fusion.1 = (f32[512]{0:T(512)S(1)}, f32[256,512]{1,0:T(8,128)S(1)}) fusion(f32[512]{0:T(512)S(1)} %bitcast.10, bf16[256,8192]{1,0:T(8,128)(2,1)} %all-gather.5.cloned.1.call-done, bf16[8192,512]{1,0:T(8,128)(2,1)} %all-gather.7.cloned.1.call-done), kind=kOutput, calls=%fused_computation.9 | convolution fusion | flops 2147876352 | bytes 13111296 | tf_op jit(solution)/shard_map/dot_general | solution.py:23
  232.0 23.9 %all-gather.1 = f32[32,1,512]{2,1,0:T(1,128)S(1)} all-gather(f32[1,1,512]{2,1,0:T(1,128)S(1)} %bitcast.11), channel_id=2, replica_groups=mesh['row'=32,'col'=16] {'row'}, dimensions={0}, use_global_device_ids=true | all-gather | bytes 67584 | tf_op jit(solution)/shard_map/all_gather | solution.py:10
  255.9 0.1 reduce_sum.29
  256.0 0.9 broadcast_multiply_fusion
  (3 shorter events, 0.0 us)
Async XLA Ops:
  6.5 141.3 %all-gather.5.cloned.1.call-start = ((), (), s32[]{:S(2)}) async-start(), calls=%async_computation | async-start | bytes 4456448 | tf_op jit(solution)/shard_map/all_gather | solution.py:27
  79.1 145.9 %all-gather.7.cloned.1.call-start = ((), (), s32[]{:S(2)}) async-start(), calls=%async_computation.1 | async-start | bytes 8650752 | tf_op jit(solution)/shard_map/all_gather | solution.py:28
Sparse Core Ops, SparseCore 0:
  79.2 68.5 all-gather.4
  151.0 73.9 all-gather.6
